TPU v7x, 128 devices: a whole 4x4x4 slice. The times are simulated.
128 devices in a mesh: node: 8 (over y_lo, z), bond: 16 (over y_hi, x, core).
Axes of the slice: x: 4, y: 4 (y_hi: 2, y_lo: 2; y = y_hi * 2 + y_lo), z: 4, core: 2. Of those that a mesh axis runs over, the one named last changes fastest.
Arguments:
- bottom_nodes: float32 [8, 128, 128, 128], P('node', 'bond'), may hold values from -0.046875 to 0.046875
- upper_nodes: float32 [8, 128, 128, 128], P(None, 'bond', 'node'), may hold values from -0.046875 to 0.046875
- leaf_up: float32 [8, 3, 2, 128, 128], P('node'), may hold values from -2 to 3
- outside_env: float32 [3, 128, 128], replicated, may hold values from -2 to 3
- top_env: float32 [3, 128, 128], replicated, may hold values from -2 to 3
Outputs:
- leaf_down: float32 [8, 3, 2, 128, 128], P('node', None, None, 'bond')
- subtree_env: float32 [3, 128, 128], replicated
All inputs are finite; a program needn't handle non-finite values.
Results may differ from a plain program's by a relative error of at most 0.0001.
Values sent between devices are 32-bit elements; how exact they have to be, the bound alone decides.
No kernel may reach another device: no remote copies, remote signals or barrier semaphores. Data moves between devices by JAX's collectives and lax.ppermute only.
A program may use at most 128 MiB of HBM per device.

v0:
```python
import jax
import jax.numpy as jnp
from jax import lax
from jax.sharding import PartitionSpec as P

highest = lax.Precision.HIGHEST


def from_everyone(x, axis):
    copies = jnp.broadcast_to(x, (lax.axis_size(axis), *x.shape))
    return lax.all_to_all(copies, axis, split_axis=0, concat_axis=0, tiled=True)


def over_copies(x, axis):
    return from_everyone(x, axis).sum(axis=0)


def in_order(pieces, dim):
    dims = list(pieces.shape[1:])
    dims[dim] *= pieces.shape[0]
    return jnp.moveaxis(pieces, 0, dim).reshape(dims)


def gather_directly(x, axis, dim):
    return in_order(from_everyone(x, axis), dim)


def packed_total(arrays, axis):
    ends = [0]
    for a in arrays:
        ends.append(ends[-1] + a.size)
    running = lax.psum(jnp.concatenate([a.ravel() for a in arrays]), axis)
    return tuple((running[b:e].reshape(a.shape) for a, b, e in zip(arrays, ends, ends[1:])))


def in_blocks(x, dim, length):
    before, after = (x.shape[:dim], x.shape[dim + 1 :])
    return jnp.moveaxis(x.reshape(*before, length, -1, *after), dim, 0)


def summed_on_arrival(x, axis, dim):
    length = lax.axis_size(axis)
    pieces = lax.all_to_all(in_blocks(x, dim, length), axis, 0, 0, tiled=True)
    return jnp.sum(pieces, axis=0)


def side_by_side(arrays, axis, dim, along):
    both = jnp.concatenate(arrays, axis=along)
    filled, at, finished = (summed_on_arrival(both, axis, dim), 0, [])
    for a in arrays:
        finished.append(lax.slice_in_dim(filled, at, at + a.shape[along], axis=along))
        at += a.shape[along]
    return tuple(finished)


def grow_product(tensor, left_env, right_env):
    middle = jnp.einsum("skac,spcd->skpad", left_env, tensor, precision=highest)
    return jnp.einsum("skpad,skbd->skpab", middle, right_env, precision=highest)


def gram_partial(tensor, product):
    return jnp.einsum("spab,skqab->skpq", tensor, product, precision=highest)


def first_part(tensor, worked, right_env):
    first = jnp.einsum("skpcd,skbd->skpcb", worked, right_env, precision=highest)
    return jnp.einsum("spab,skpcb->skac", tensor, first, precision=highest)


def second_part(tensor, worked, left_env):
    second = jnp.einsum("skac,skpcd->skpad", left_env, worked, precision=highest)
    return jnp.einsum("spab,skpad->skbd", tensor, second, precision=highest)


def upper_up(columns, parents, left_env, right_env):
    middle = jnp.einsum("skac,spcd->skpad", left_env, columns, precision=highest)
    middle_rows = lax.all_to_all(middle, "node", split_axis=3, concat_axis=4, tiled=True)
    product = jnp.einsum("skpad,skbd->skpab", middle_rows, right_env, precision=highest)
    product_all = lax.all_to_all(product, "bond", split_axis=4, concat_axis=2, tiled=True)
    return lax.psum(gram_partial(parents, product_all), ("node", "bond"))


def down_parts(columns, parents, above, left_env, right_env, with_second):
    worked_all = jnp.einsum("skpq,sqcd->skpcd", above, parents, precision=highest)
    worked = lax.all_to_all(worked_all, "bond", split_axis=2, concat_axis=4, tiled=True)
    first_rows = jnp.einsum("skpcd,skbd->skpcb", worked, right_env, precision=highest)
    first_cols = lax.all_to_all(first_rows, "node", split_axis=4, concat_axis=3, tiled=True)
    first_env = jnp.einsum("spab,skpcb->skac", columns, first_cols, precision=highest)
    if not with_second:
        return (first_env,)
    side = jnp.einsum("spab,skac->skpcb", columns, left_env, precision=highest)
    side_rows = lax.all_to_all(side, "node", split_axis=3, concat_axis=4, tiled=True)
    second_env = jnp.einsum("skpcb,skpcd->skbd", side_rows, worked, precision=highest)
    return (first_env, second_env)


def local(bottom_nodes, upper_nodes, leaf_up, outside_env, top_env):
    nodes = lax.axis_size("node")
    width = bottom_nodes.shape[2]
    rows = bottom_nodes.shape[1]
    operators = leaf_up.shape[1]
    left_leaf = leaf_up[:, :, 0]
    right_leaf = leaf_up[:, :, 1]
    product = grow_product(bottom_nodes, left_leaf, right_leaf)
    tensor_a = lax.all_to_all(bottom_nodes, "bond", split_axis=2, concat_axis=1, tiled=True)
    product_a = lax.all_to_all(product, "bond", split_axis=3, concat_axis=2, tiled=True)
    own_env = over_copies(gram_partial(tensor_a, product_a), "bond")
    children = gather_directly(own_env, "node", 0)
    upper_cols = lax.all_to_all(upper_nodes, "node", split_axis=3, concat_axis=2, tiled=True)
    upper_pars = lax.all_to_all(upper_nodes, "bond", split_axis=3, concat_axis=1, tiled=True)
    ups = {nodes: children}
    level_size = nodes // 2
    while level_size >= 1:
        below = ups[2 * level_size]
        ups[level_size] = upper_up(
            upper_cols[level_size : 2 * level_size],
            upper_pars[level_size : 2 * level_size],
            below[0::2],
            below[1::2],
        )
        level_size = level_size // 2
    root_env = ups[1]
    crown_part = down_parts(
        upper_cols[0:1], upper_pars[0:1], top_env[None], root_env, outside_env[None], False
    )[0]
    above = lax.psum(crown_part, ("node", "bond"))
    level_size = 1
    while level_size < nodes:
        below = ups[2 * level_size]
        first_env, second_env = down_parts(
            upper_cols[level_size : 2 * level_size],
            upper_pars[level_size : 2 * level_size],
            above,
            below[0::2],
            below[1::2],
            True,
        )
        first_env, second_env = packed_total((first_env, second_env), ("node", "bond"))
        above = jnp.stack([first_env, second_env], 1).reshape(
            2 * level_size, operators, width, width
        )
        level_size = level_size * 2
    mine = lax.dynamic_index_in_dim(above, lax.axis_index("node"), 0, keepdims=True)
    own_rows = lax.dynamic_slice_in_dim(mine, lax.axis_index("bond") * rows, rows, 2)
    worked = jnp.einsum(
        "skpq,sqcd->skpcd",
        own_rows,
        lax.all_gather(bottom_nodes, "bond", axis=1, tiled=True),
        precision=highest,
    )
    first_env = first_part(bottom_nodes, worked, right_leaf)
    second_env = second_part(bottom_nodes, worked, left_leaf)
    first_env, second_env = side_by_side((first_env, second_env), "bond", 2, 0)
    leaf_down = jnp.stack([first_env, second_env], 2)
    return (leaf_down, root_env[0])


def solution(mesh):
    placed = (
        P("node", "bond", None, None),
        P(None, "bond", "node", None),
        P("node", None, None, None, None),
        P(),
        P(),
    )
    return jax.shard_map(
        local,
        mesh=mesh,
        in_specs=placed,
        out_specs=(P("node", None, None, "bond", None), P()),
        check_vma=False,
    )
```

profile of v0, /device:TPU:1, one launch (start us, length us, event | category | flops | bytes accessed | tf_op | source)
XLA Modules:
  0.0 1421.0 jit_solution(13063152270408654019)
XLA Ops:
  10.3 8.4 all-to-all-start.6
  29.7 26.2 %all_to_all.360 = f32[1,3,8,128,128]{4,2,1,0,3:T(8,128)S(1)} all-to-all(f32[1,3,8,128,128]{4,2,1,0,3:T(8,128)S(1)} %copy.237), channel_id=1, replica_groups=mesh['node'=8,'bond'=16] {'bond'}, dimensions={3} | all-to-all | bytes 3145728 | tf_op jit(solution)/shard_map/all_to_all | solution.py:106
  74.2 31.9 %all-to-all-done.7 = f32[16,1,3,128,128]{4,3,2,1,0:T(8,128)S(1)} async-done(((f32[16,1,3,128,128]{4,3,2,1,0:T(8,128)}), f32[16,1,3,128,128]{4,3,2,1,0:T(8,128)S(1)}, u32[]{:S(2)}, u32[]{:S(2)}) %all-to-all-start.7) | async-done | bytes 3145760 | tf_op jit(solution)/shard_map/all_to_all | solution.py:11
  111.4 7.7 all-to-all-done.3
  147.5 6.0 copy.242
  166.7 7.5 all-to-all-done.9
  174.3 7.8 all-to-all-start
  189.3 9.0 copy.468
  215.9 7.2 all-to-all-start.10
  243.9 6.4 copy.246
  250.3 6.7 fusion.39
  263.2 6.8 all-to-all-start.1
  270.0 134.2 %all-reduce.8.cloned.1.call-done = f32[4,3,128,128]{2,3,1,0:T(8,128)} async-done(((f32[4,3,128,128]{2,3,1,0:T(8,128)}), f32[4,3,128,128]{2,3,1,0:T(8,128)}) %all-reduce.8.cloned.1.call-update) | async-done | bytes 786448 | tf_op jit(solution)/shard_map/psum | solution.py:80
  443.8 6.1 all-to-all-start.12
  470.1 147.5 %all-reduce.16.cloned.1.call-done = (f32[2,3,128,128]{2,3,1,0:T(8,128)}, f32[3,128,128]{1,2,0:T(8,128)}) async-done(((f32[2,3,128,128]{2,3,1,0:T(8,128)}, f32[3,128,128]{1,2,0:T(8,128)}), (f32[2,3,128,128]{2,3,1,0:T(8,128)}, f32[3,128,128]{1,2,0:T(8,128)})) %all-reduce.16.cloned.1.call-update) | async-done | bytes 589840 | tf_op jit(solution)/shard_map/psum | solution.py:80
  630.7 6.9 all-to-all-start.4
  669.1 142.6 %all-reduce.10.cloned.1.call-done = f32[98304]{0:T(1024)} async-done(((f32[98304]{0:T(1024)}), f32[98304]{0:T(1024)}) %all-reduce.10.cloned.1.call-update) | async-done | bytes 393232 | tf_op jit(solution)/shard_map/psum | solution.py:32
  818.0 6.2 all-to-all-start.15
  843.7 6.8 fusion.12
  877.8 6.9 fusion.10
  905.6 139.7 %all-reduce.12.cloned.1.call-done = f32[196608]{0:T(1024)} async-done(((f32[196608]{0:T(1024)}), f32[196608]{0:T(1024)}) %all-reduce.12.cloned.1.call-update) | async-done | bytes 786448 | tf_op jit(solution)/shard_map/psum | solution.py:32
  1059.1 6.3 all-to-all-start.18
  1099.3 6.2 all-to-all-start.23
  1105.5 11.9 fusion.4
  1117.5 6.0 copy.287
  1142.4 9.0 copy.466
  1161.1 12.4 fusion.2
  1180.7 9.0 copy.467
  1199.3 178.5 %all-reduce.14.cloned.1.call-done = (f32[393216]{0:T(1024)}, f32[3,128,128]{1,2,0:T(8,128)}) async-done(((f32[393216]{0:T(1024)}, f32[3,128,128]{1,2,0:T(8,128)}), (f32[393216]{0:T(1024)}, f32[3,128,128]{1,2,0:T(8,128)})) %all-reduce.14.cloned.1.call-update) | async-done | bytes 1769488 | tf_op jit(solution)/shard_map/psum | solution.py:32
  1379.5 7.5 fusion
  1397.0 6.3 all-to-all-start.21
  1404.1 8.9 all-to-all-done.21
  (276 shorter events, 413.8 us)
Async XLA Ops:
  8.0 253.0 %copy-start = (f32[3,128,128]{2,1,0:T(8,128)S(1)}, f32[3,128,128]{2,1,0:T(8,128)}, u32[]{:S(2)}) copy-start(f32[3,128,128]{2,1,0:T(8,128)} %param.9) | copy-start | bytes 589828
  10.3 19.4 %all-to-all-start.6 = ((f32[1,8,128,128]{3,1,0,2:T(8,128)}), f32[1,8,128,128]{3,1,0,2:T(8,128)S(1)}, u32[]{:S(2)}, u32[]{:S(2)}) async-start(f32[1,8,128,128]{3,1,0,2:T(8,128)} %copy.239), calls=%async_computation.6 | async-start | bytes 1048576 | tf_op jit(solution)/shard_map/all_to_all | solution.py:105
  59.5 46.6 %all-to-all-start.7 = ((f32[16,1,3,128,128]{4,3,2,1,0:T(8,128)}), f32[16,1,3,128,128]{4,3,2,1,0:T(8,128)S(1)}, u32[]{:S(2)}, u32[]{:S(2)}) async-start(f32[16,1,3,128,128]{4,3,2,1,0:T(8,128)} %broadcast_in_dim.8), calls=%async_computation.7 | async-start | bytes 6291456 | tf_op jit(solution)/shard_map/all_to_all | solution.py:11
  106.1 13.0 all-to-all-start.3
  120.5 26.0 %all-to-all-start.8 = ((f32[8,1,3,128,128]{4,3,2,1,0:T(8,128)}), f32[8,1,3,128,128]{4,3,2,1,0:T(8,128)S(1)}, u32[]{:S(2)}, u32[]{:S(2)}) async-start(f32[8,1,3,128,128]{4,3,2,1,0:T(8,128)} %broadcast_in_dim.9), calls=%async_computation.8 | async-start | bytes 3145728 | tf_op jit(solution)/shard_map/all_to_all | solution.py:11
  146.5 56.2 %copy-start.4 = (f32[8,1,3,128,128]{4,3,2,1,0:T(8,128)}, f32[8,1,3,128,128]{4,3,2,1,0:T(8,128)S(1)}, u32[]{:S(2)}) copy-start(f32[8,1,3,128,128]{4,3,2,1,0:T(8,128)S(1)} %all-to-all-done.8) | copy-start | bytes 4718596
  158.9 15.3 %all-to-all-start.9 = ((f32[8,1,24576]{2,1,0:T(1,128)}), f32[8,1,24576]{2,1,0:T(1,128)S(1)}, u32[]{:S(2)}, u32[]{:S(2)}) async-start(f32[8,1,24576]{2,1,0:T(1,128)} %reshape.318), calls=%async_computation.9 | async-start | bytes 1572864 | tf_op jit(solution)/shard_map/all_to_all | solution.py:77
  174.3 41.6 %all-to-all-start = ((f32[16,1,8192]{2,1,0:T(1,128)}), f32[16,1,8192]{2,1,0:T(1,128)}, u32[]{:S(2)}, u32[]{:S(2)}) async-start(f32[16,1,8192]{2,1,0:T(1,128)} %reshape.316), calls=%async_computation | async-start | bytes 1048576 | tf_op jit(solution)/shard_map/all_to_all | solution.py:110
  215.9 21.5 %all-to-all-start.10 = ((f32[16,1,12288]{2,1,0:T(1,128)}), f32[16,1,12288]{2,1,0:T(1,128)S(1)}, u32[]{:S(2)}, u32[]{:S(2)}) async-start(f32[16,1,12288]{2,1,0:T(1,128)} %reshape.320), calls=%async_computation.10 | async-start | bytes 1572864 | tf_op jit(solution)/shard_map/all_to_all | solution.py:79
  223.1 181.1 %all-reduce.8.cloned.1.call-start = ((), (), s32[]{:S(2)}) async-start(), calls=%async_computation.24 | async-start | bytes 1572864 | tf_op jit(solution)/shard_map/psum | solution.py:80
  263.2 147.2 %all-to-all-start.1 = ((f32[16,1,3072]{2,1,0:T(1,128)}), f32[16,1,3072]{2,1,0:T(1,128)S(1)}, u32[]{:S(2)}, u32[]{:S(2)}) async-start(f32[16,1,3072]{2,1,0:T(1,128)} %reshape.330), calls=%async_computation.1 | async-start | bytes 393216 | tf_op jit(solution)/shard_map/all_to_all | solution.py:85
  411.1 11.9 all-to-all-start.11
  423.0 20.8 %all-to-all-start.2 = ((f32[8,1,6144]{2,1,0:T(1,128)}), f32[8,1,6144]{2,1,0:T(1,128)S(1)}, u32[]{:S(2)}, u32[]{:S(2)}) async-start(f32[8,1,6144]{2,1,0:T(1,128)} %reshape.332), calls=%async_computation.2 | async-start | bytes 393216 | tf_op jit(solution)/shard_map/all_to_all | solution.py:87
  443.8 15.9 %all-to-all-start.12 = ((f32[16,1,6144]{2,1,0:T(1,128)}), f32[16,1,6144]{2,1,0:T(1,128)}, u32[]{:S(2)}, u32[]{:S(2)}) async-start(f32[16,1,6144]{2,1,0:T(1,128)} %reshape.326), calls=%async_computation.12 | async-start | bytes 786432 | tf_op jit(solution)/shard_map/all_to_all | solution.py:79
  450.0 167.6 %all-reduce.16.cloned.1.call-start = ((), (), s32[]{:S(2)}) async-start(), calls=%async_computation.29 | async-start | bytes 1179648 | tf_op jit(solution)/shard_map/psum | solution.py:80
  620.7 10.0 all-to-all-start.14
  630.7 15.1 %all-to-all-start.4 = ((f32[16,1,3072]{2,1,0:T(1,128)}), f32[16,1,3072]{2,1,0:T(1,128)}, u32[]{:S(2)}, u32[]{:S(2)}) async-start(f32[16,1,3072]{2,1,0:T(1,128)} %reshape.334), calls=%async_computation.4 | async-start | bytes 393216 | tf_op jit(solution)/shard_map/all_to_all | solution.py:85
  655.4 9.2 all-to-all-start.13
  658.8 152.9 %all-reduce.10.cloned.1.call-start = ((), (), s32[]{:S(2)}) async-start(), calls=%async_computation.25 | async-start | bytes 786432 | tf_op jit(solution)/shard_map/psum | solution.py:32
  818.0 15.9 %all-to-all-start.15 = ((f32[16,1,6144]{2,1,0:T(1,128)}), f32[16,1,6144]{2,1,0:T(1,128)}, u32[]{:S(2)}, u32[]{:S(2)}) async-start(f32[16,1,6144]{2,1,0:T(1,128)} %reshape.338), calls=%async_computation.15 | async-start | bytes 786432 | tf_op jit(solution)/shard_map/all_to_all | solution.py:85
  834.0 23.0 %all-to-all-start.17 = ((f32[8,1,12288]{2,1,0:T(1,128)}), f32[8,1,12288]{2,1,0:T(1,128)}, u32[]{:S(2)}, u32[]{:S(2)}) async-start(f32[8,1,12288]{2,1,0:T(1,128)} %reshape.322), calls=%async_computation.17 | async-start | bytes 786432 | tf_op jit(solution)/shard_map/all_to_all | solution.py:92
  857.0 27.7 %all-to-all-start.16 = ((f32[8,1,12288]{2,1,0:T(1,128)}), f32[8,1,12288]{2,1,0:T(1,128)}, u32[]{:S(2)}, u32[]{:S(2)}) async-start(f32[8,1,12288]{2,1,0:T(1,128)} %reshape.340), calls=%async_computation.16 | async-start | bytes 786432 | tf_op jit(solution)/shard_map/all_to_all | solution.py:87
  862.1 183.2 %all-reduce.12.cloned.1.call-start = ((), (), s32[]{:S(2)}) async-start(), calls=%async_computation.26 | async-start | bytes 1572864 | tf_op jit(solution)/shard_map/psum | solution.py:32
  900.5 158.6 %all-to-all-start.22 = ((f32[8,1,6144]{2,1,0:T(1,128)}), f32[8,1,6144]{2,1,0:T(1,128)S(1)}, u32[]{:S(2)}, u32[]{:S(2)}) async-start(f32[8,1,6144]{2,1,0:T(1,128)} %reshape.346), calls=%async_computation.22 | async-start | bytes 393216 | tf_op jit(solution)/shard_map/all_to_all | solution.py:77
  905.6 141.0 %copy-start.13 = (f32[4,128,16,8,1]{1,2,3,4,0:T(8,128)S(1)}, f32[4,128,16,8,1]{1,2,3,4,0:T(8,128)}, u32[]{:S(2)}) copy-start(f32[4,128,16,8,1]{1,2,3,4,0:T(8,128)} %copy-done.12) | copy-start | bytes 786436
  1059.1 20.6 %all-to-all-start.18 = ((f32[16,1,12288]{2,1,0:T(1,128)}), f32[16,1,12288]{2,1,0:T(1,128)S(1)}, u32[]{:S(2)}, u32[]{:S(2)}) async-start(f32[16,1,12288]{2,1,0:T(1,128)} %reshape.342), calls=%async_computation.18 | async-start | bytes 1572864 | tf_op jit(solution)/shard_map/all_to_all | solution.py:85
  1079.6 19.7 %all-to-all-start.20 = ((f32[8,1,24576]{2,1,0:T(1,128)}), f32[8,1,24576]{2,1,0:T(1,128)}, u32[]{:S(2)}, u32[]{:S(2)}) async-start(f32[8,1,24576]{2,1,0:T(1,128)} %reshape.314), calls=%async_computation.20 | async-start | bytes 1572864 | tf_op jit(solution)/shard_map/all_to_all | solution.py:92
  1099.3 29.6 %all-to-all-start.23 = ((f32[16,1,3072]{2,1,0:T(1,128)}), f32[16,1,3072]{2,1,0:T(1,128)S(1)}, u32[]{:S(2)}, u32[]{:S(2)}) async-start(f32[16,1,3072]{2,1,0:T(1,128)} %reshape.348), calls=%async_computation.23 | async-start | bytes 393216 | tf_op jit(solution)/shard_map/all_to_all | solution.py:79
  1129.0 44.5 %all-to-all-start.19 = ((f32[8,1,24576]{2,1,0:T(1,128)}), f32[8,1,24576]{2,1,0:T(1,128)S(1)}, u32[]{:S(2)}, u32[]{:S(2)}) async-start(f32[8,1,24576]{2,1,0:T(1,128)} %reshape.344), calls=%async_computation.19 | async-start | bytes 1572864 | tf_op jit(solution)/shard_map/all_to_all | solution.py:87
  1133.8 244.0 %all-reduce.14.cloned.1.call-start = ((), (), s32[]{:S(2)}) async-start(), calls=%async_computation.28 | async-start | bytes 3538944 | tf_op jit(solution)/shard_map/psum | solution.py:32
  1197.1 182.3 %all-gather.2.cloned.1.call-start = ((), (), s32[]{:S(2)}) async-start(), calls=%async_computation.27 | async-start | bytes 8912896 | tf_op jit(solution)/shard_map/all_gather | solution.py:148
  1397.0 15.9 %all-to-all-start.21 = ((f32[16,2,3,8,128]{4,3,2,1,0:T(8,128)}), f32[16,2,3,8,128]{4,3,2,1,0:T(8,128)S(1)}, u32[]{:S(2)}, u32[]{:S(2)}) async-start(f32[16,2,3,8,128]{4,3,2,1,0:T(8,128)} %copy_bitcast_fusion.13), calls=%async_computation.21 | async-start | bytes 786432 | tf_op jit(solution)/shard_map/all_to_all | solution.py:43
  (28 other events, 134.0 us)
Sparse Core Ops, SparseCore 0:
  257.1 147.0 all-reduce.7
  470.0 147.5 all-reduce.15
  669.2 142.3 all-reduce.9
  898.5 146.7 all-reduce.11
  1197.2 180.5 all-reduce.13
Sparse Core Ops, SparseCore 1:
  1199.9 81.7 all-gather.1
where the time goes:
time: 1430 us; the launch traced here: 1420 us
  waiting for transfers between devices  823 us (58%)
  local copies, waits for them, and re-layouts  275 us (19%)
  starting transfers between devices  129 us (9%)
  matrix products  101 us (7%)
  other arithmetic  50.9 us (4%)
  blocking collectives  26.2 us (2%)
  between operations  16.5 us (1%)
    psum x3, waiting for transfers between devices, packed_total(): running = lax.psum(jnp.concatenate([a.ravel() for a in arrays]), axis)  461 us
    psum x2, waiting for transfers between devices, upper_up(): return lax.psum(gram_partial(parents, product_all), ('node', 'bond'))  282 us
    unnamed x104, local copies, waits for them, and re-layouts  117 us
    all_to_all x2, waiting for transfers between devices, from_everyone(): return lax.all_to_all(copies, axis, split_axis=0, concat_axis=0, tiled=True)  35.4 us
  transfers between devices with their start and end apart: 29, of which 18 were waited for; matrix products, arithmetic and copies ran while one was open for 19% of the time, Pallas kernels for 0%

commit v1 on v0

--- a/solution.py
+++ b/solution.py
@@ -77,7 +77,7 @@
     middle_rows = lax.all_to_all(middle, "node", split_axis=3, concat_axis=4, tiled=True)
     product = jnp.einsum("skpad,skbd->skpab", middle_rows, right_env, precision=highest)
     product_all = lax.all_to_all(product, "bond", split_axis=4, concat_axis=2, tiled=True)
-    return lax.psum(gram_partial(parents, product_all), ("node", "bond"))
+    return lax.psum(lax.psum(gram_partial(parents, product_all), "bond"), "node")
 
 
 def down_parts(columns, parents, above, left_env, right_env, with_second):

time: 1430 us -> 1940 us (1.36)
  waiting for transfers between devices: 823 us -> 1290 us
  blocking collectives: 26.2 us -> 50.9 us
    psum x2 -> x7, waiting for transfers between devices: 282 us -> 735 us  [the longest x3 384 us: upper_up(): lax.psum(gram_partial(parents, product_all), 'bond')]
    all_gather x1, waiting for transfers between devices: 0.03 us -> 78.5 us  [local(): lax.all_gather(bottom_nodes, 'bond', axis=1, tiled=True)]
    psum x3, waiting for transfers between devices: 461 us -> 408 us  [packed_total(): running = lax.psum(jnp.concatenate([a.ravel() for a in arrays]), axis)]
    all_to_all x0 -> x2, blocking collectives: none -> 24.7 us  [the longest x1 14.1 us: down_parts(): lax.all_to_all(worked_all, 'bond', split_axis=2, concat_axis=4, tiled=True)]
    unnamed x104 -> x90, local copies, waits for them, and re-layouts: 117 us -> 117 us
  transfers between devices with their start and end apart: 29 -> 32, of which waited for: 18 -> 21; matrix products, arithmetic and copies ran while one was open for 19% -> 15% of each run, Pallas kernels for 0% -> 0%
where the time goes in v1:
time: 1940 us; the launch traced here: 1920 us
  waiting for transfers between devices  1290 us (66%)
  local copies, waits for them, and re-layouts  281 us (14%)
  starting transfers between devices  125 us (6%)
  matrix products  102 us (5%)
  other arithmetic  51.9 us (3%)
  blocking collectives  50.9 us (3%)
    psum x3, waiting for transfers between devices, packed_total(): running = lax.psum(jnp.concatenate([a.ravel() for a in arrays]), axis)  408 us
    psum x3, waiting for transfers between devices, upper_up(): lax.psum(gram_partial(parents, product_all), 'bond')  384 us
    psum x3, waiting for transfers between devices, upper_up(): lax.psum(lax.psum(gram_partial(parents, product_all), 'bond'), 'node')  200 us
    psum x1, waiting for transfers between devices, local(): above = lax.psum(crown_part, ('node', 'bond'))  150 us
    unnamed x90, local copies, waits for them, and re-layouts  117 us
    all_gather x1, waiting for transfers between devices, local(): lax.all_gather(bottom_nodes, 'bond', axis=1, tiled=True)  78.5 us
  transfers between devices with their start and end apart: 32, of which 21 were waited for; matrix products, arithmetic and copies ran while one was open for 15% of the time, Pallas kernels for 0%

profile of v1, /device:TPU:1, one launch (start us, length us, event | category | flops | bytes accessed | tf_op | source)
XLA Modules:
  0.0 1918.8 jit_solution(7512533263398065860)
XLA Ops:
  9.4 8.4 all-to-all-start.6
  28.9 26.2 %all_to_all.360 = f32[1,3,8,128,128]{4,2,1,0,3:T(8,128)S(1)} all-to-all(f32[1,3,8,128,128]{4,2,1,0,3:T(8,128)S(1)} %copy.237), channel_id=1, replica_groups=mesh['node'=8,'bond'=16] {'bond'}, dimensions={3} | all-to-all | bytes 3145728 | tf_op jit(solution)/shard_map/all_to_all | solution.py:106
  73.2 32.0 %all-to-all-done.7 = f32[16,1,3,128,128]{4,3,2,1,0:T(8,128)S(1)} async-done(((f32[16,1,3,128,128]{4,3,2,1,0:T(8,128)}), f32[16,1,3,128,128]{4,3,2,1,0:T(8,128)S(1)}, u32[]{:S(2)}, u32[]{:S(2)}) %all-to-all-start.7) | async-done | bytes 3145760 | tf_op jit(solution)/shard_map/all_to_all | solution.py:11
  110.5 7.7 all-to-all-done.3
  165.9 7.5 all-to-all-done.9
  173.4 7.8 all-to-all-start
  188.5 9.1 copy.468
  215.1 7.2 all-to-all-start.10
  256.2 139.2 %all-reduce.13.cloned.1.call-done = f32[4,3,128,128]{2,3,1,0:T(8,128)} async-done(((f32[4,3,128,128]{2,3,1,0:T(8,128)}), f32[4,3,128,128]{2,3,1,0:T(8,128)}) %all-reduce.13.cloned.1.call-update) | async-done | bytes 786448 | tf_op jit(solution)/shard_map/psum | solution.py:80
  397.0 73.3 %all-reduce.15.cloned.1.call-done = f32[4,3,128,128]{2,3,1,0:T(8,128)} async-done(((f32[4,3,128,128]{2,3,1,0:T(8,128)}), f32[4,3,128,128]{2,3,1,0:T(8,128)}) %all-reduce.15.cloned.1.call-update) | async-done | bytes 786448 | tf_op jit(solution)/shard_map/psum | solution.py:80
  486.7 13.4 all-to-all-start.1
  515.8 7.7 all-to-all-start.12
  554.1 133.0 %all-reduce.17.cloned.1.call-done = f32[2,3,128,128]{2,3,1,0:T(8,128)} async-done(((f32[2,3,128,128]{2,3,1,0:T(8,128)}), f32[2,3,128,128]{2,3,1,0:T(8,128)}) %all-reduce.17.cloned.1.call-update) | async-done | bytes 393232 | tf_op jit(solution)/shard_map/psum | solution.py:80
  687.4 150.5 %all-reduce.11.cloned.1.call-done = f32[3,128,128]{1,2,0:T(8,128)} async-done(((f32[3,128,128]{1,2,0:T(8,128)}), f32[3,128,128]{1,2,0:T(8,128)}) %all-reduce.11.cloned.1.call-update) | async-done | bytes 196624 | tf_op jit(solution)/shard_map/psum | solution.py:126
  840.2 14.1 all_to_all.361
  856.0 53.4 %all-reduce.19.cloned.1.call-done = f32[2,3,128,128]{2,3,1,0:T(8,128)} async-done(((f32[2,3,128,128]{2,3,1,0:T(8,128)}), f32[2,3,128,128]{2,3,1,0:T(8,128)}) %all-reduce.19.cloned.1.call-update) | async-done | bytes 393232 | tf_op jit(solution)/shard_map/psum | solution.py:80
  952.7 152.7 %all-reduce.21.cloned.1.call-done = f32[98304]{0:T(1024)} async-done(((f32[98304]{0:T(1024)}), f32[98304]{0:T(1024)}) %all-reduce.21.cloned.1.call-update) | async-done | bytes 393232 | tf_op jit(solution)/shard_map/psum | solution.py:32
  1137.6 6.8 fusion.12
  1171.6 6.9 fusion.10
  1191.9 146.4 %all-reduce.23.cloned.1.call-done = f32[196608]{0:T(1024)} async-done(((f32[196608]{0:T(1024)}), f32[196608]{0:T(1024)}) %all-reduce.23.cloned.1.call-update) | async-done | bytes 786448 | tf_op jit(solution)/shard_map/psum | solution.py:32
  1385.0 11.9 fusion.4
  1421.0 9.0 copy.466
  1434.3 12.4 fusion.2
  1454.1 9.1 copy.467
  1474.1 10.7 all_to_all.362
  1492.6 8.5 all-to-all-start.23
  1501.2 8.1 all-to-all-done.23
  1513.6 109.0 %all-reduce.25.cloned.1.call-done = f32[393216]{0:T(1024)} async-done(((f32[393216]{0:T(1024)}), f32[393216]{0:T(1024)}) %all-reduce.25.cloned.1.call-update) | async-done | bytes 1572880 | tf_op jit(solution)/shard_map/psum | solution.py:32
  1624.3 78.5 %all-gather.2.cloned.1.call-done = f32[1,128,128,128]{3,1,2,0:T(8,128)} async-done(((f32[1,8,128,128]{3,1,2,0:T(8,128)}), f32[1,128,128,128]{3,1,2,0:T(8,128)}) %all-gather.2.cloned.1.call-update) | async-done | bytes 8388624 | tf_op jit(solution)/shard_map/all_gather | solution.py:148
  1702.8 7.4 fusion
  1723.8 112.3 %all-reduce.27.cloned.1.call-done = f32[1,3,128,128]{2,3,1,0:T(8,128)} async-done(((f32[1,3,128,128]{2,3,1,0:T(8,128)}), f32[1,3,128,128]{2,3,1,0:T(8,128)}) %all-reduce.27.cloned.1.call-update) | async-done | bytes 196624 | tf_op jit(solution)/shard_map/psum | solution.py:80
  1836.2 73.5 %all-reduce.29.cloned.1.call-done = f32[3,128,128]{1,2,0:T(8,128)} async-done(((f32[3,128,128]{1,2,0:T(8,128)}), f32[3,128,128]{1,2,0:T(8,128)}) %all-reduce.29.cloned.1.call-update) | async-done | bytes 196624 | tf_op jit(solution)/shard_map/psum | solution.py:80
  (275 shorter events, 450.0 us)
Async XLA Ops:
  9.4 19.4 %all-to-all-start.6 = ((f32[1,8,128,128]{3,1,0,2:T(8,128)}), f32[1,8,128,128]{3,1,0,2:T(8,128)S(1)}, u32[]{:S(2)}, u32[]{:S(2)}) async-start(f32[1,8,128,128]{3,1,0,2:T(8,128)} %copy.239), calls=%async_computation.6 | async-start | bytes 1048576 | tf_op jit(solution)/shard_map/all_to_all | solution.py:105
  58.6 46.6 %all-to-all-start.7 = ((f32[16,1,3,128,128]{4,3,2,1,0:T(8,128)}), f32[16,1,3,128,128]{4,3,2,1,0:T(8,128)S(1)}, u32[]{:S(2)}, u32[]{:S(2)}) async-start(f32[16,1,3,128,128]{4,3,2,1,0:T(8,128)} %broadcast_in_dim.8), calls=%async_computation.7 | async-start | bytes 6291456 | tf_op jit(solution)/shard_map/all_to_all | solution.py:11
  105.2 13.0 all-to-all-start.3
  119.6 26.0 %all-to-all-start.8 = ((f32[8,1,3,128,128]{4,3,2,1,0:T(8,128)}), f32[8,1,3,128,128]{4,3,2,1,0:T(8,128)S(1)}, u32[]{:S(2)}, u32[]{:S(2)}) async-start(f32[8,1,3,128,128]{4,3,2,1,0:T(8,128)} %broadcast_in_dim.9), calls=%async_computation.8 | async-start | bytes 3145728 | tf_op jit(solution)/shard_map/all_to_all | solution.py:11
  158.1 15.3 all-to-all-start.9
  173.4 41.7 %all-to-all-start = ((f32[16,1,8192]{2,1,0:T(1,128)}), f32[16,1,8192]{2,1,0:T(1,128)}, u32[]{:S(2)}, u32[]{:S(2)}) async-start(f32[16,1,8192]{2,1,0:T(1,128)} %reshape.316), calls=%async_computation | async-start | bytes 1048576 | tf_op jit(solution)/shard_map/all_to_all | solution.py:110
  215.1 21.5 %all-to-all-start.10 = ((f32[16,1,12288]{2,1,0:T(1,128)}), f32[16,1,12288]{2,1,0:T(1,128)S(1)}, u32[]{:S(2)}, u32[]{:S(2)}) async-start(f32[16,1,12288]{2,1,0:T(1,128)} %reshape.320), calls=%async_computation.10 | async-start | bytes 1572864 | tf_op jit(solution)/shard_map/all_to_all | solution.py:79
  222.3 173.1 %all-reduce.13.cloned.1.call-start = ((), (), s32[]{:S(2)}) async-start(), calls=%async_computation.25 | async-start | bytes 1572864 | tf_op jit(solution)/shard_map/psum | solution.py:80
  256.2 214.2 %all-reduce.15.cloned.1.call-start = ((), (), s32[]{:S(2)}) async-start(), calls=%async_computation.26 | async-start | bytes 1572864 | tf_op jit(solution)/shard_map/psum | solution.py:80
  476.7 10.0 all-to-all-start.11
  486.7 29.1 %all-to-all-start.1 = ((f32[16,1,3072]{2,1,0:T(1,128)}), f32[16,1,3072]{2,1,0:T(1,128)S(1)}, u32[]{:S(2)}, u32[]{:S(2)}) async-start(f32[16,1,3072]{2,1,0:T(1,128)} %reshape.330), calls=%async_computation.1 | async-start | bytes 393216 | tf_op jit(solution)/shard_map/all_to_all | solution.py:85
  515.8 17.4 all-to-all-start.12
  533.3 15.7 all-to-all-start.2
  537.3 149.8 %all-reduce.17.cloned.1.call-start = ((), (), s32[]{:S(2)}) async-start(), calls=%async_computation.27 | async-start | bytes 786432 | tf_op jit(solution)/shard_map/psum | solution.py:80
  546.4 291.4 %all-reduce.11.cloned.1.call-start = ((), (), s32[]{:S(2)}) async-start(), calls=%async_computation.24 | async-start | bytes 393216 | tf_op jit(solution)/shard_map/psum | solution.py:126
  554.1 355.4 %all-reduce.19.cloned.1.call-start = ((), (), s32[]{:S(2)}) async-start(), calls=%async_computation.28 | async-start | bytes 786432 | tf_op jit(solution)/shard_map/psum | solution.py:80
  916.3 10.0 all-to-all-start.13
  926.3 14.7 all-to-all-start.14
  931.4 173.9 %all-reduce.21.cloned.1.call-start = ((), (), s32[]{:S(2)}) async-start(), calls=%async_computation.29 | async-start | bytes 786432 | tf_op jit(solution)/shard_map/psum | solution.py:32
  1111.7 16.4 all-to-all-start.15
  1128.1 22.8 %all-to-all-start.17 = ((f32[8,1,12288]{2,1,0:T(1,128)}), f32[8,1,12288]{2,1,0:T(1,128)}, u32[]{:S(2)}, u32[]{:S(2)}) async-start(f32[8,1,12288]{2,1,0:T(1,128)} %reshape.322), calls=%async_computation.17 | async-start | bytes 786432 | tf_op jit(solution)/shard_map/all_to_all | solution.py:92
  1150.9 27.6 %all-to-all-start.16 = ((f32[8,1,12288]{2,1,0:T(1,128)}), f32[8,1,12288]{2,1,0:T(1,128)}, u32[]{:S(2)}, u32[]{:S(2)}) async-start(f32[8,1,12288]{2,1,0:T(1,128)} %reshape.340), calls=%async_computation.16 | async-start | bytes 786432 | tf_op jit(solution)/shard_map/all_to_all | solution.py:87
  1155.9 182.4 %all-reduce.23.cloned.1.call-start = ((), (), s32[]{:S(2)}) async-start(), calls=%async_computation.30 | async-start | bytes 1572864 | tf_op jit(solution)/shard_map/psum | solution.py:32
  1352.1 20.6 %all-to-all-start.18 = ((f32[16,1,12288]{2,1,0:T(1,128)}), f32[16,1,12288]{2,1,0:T(1,128)S(1)}, u32[]{:S(2)}, u32[]{:S(2)}) async-start(f32[16,1,12288]{2,1,0:T(1,128)} %reshape.342), calls=%async_computation.18 | async-start | bytes 1572864 | tf_op jit(solution)/shard_map/all_to_all | solution.py:85
  1373.6 34.9 %all-to-all-start.20 = ((f32[8,1,24576]{2,1,0:T(1,128)}), f32[8,1,24576]{2,1,0:T(1,128)S(1)}, u32[]{:S(2)}, u32[]{:S(2)}) async-start(f32[8,1,24576]{2,1,0:T(1,128)} %reshape.314), calls=%async_computation.20 | async-start | bytes 1572864 | tf_op jit(solution)/shard_map/all_to_all | solution.py:92
  1408.4 38.3 %all-to-all-start.19 = ((f32[8,1,24576]{2,1,0:T(1,128)}), f32[8,1,24576]{2,1,0:T(1,128)S(1)}, u32[]{:S(2)}, u32[]{:S(2)}) async-start(f32[8,1,24576]{2,1,0:T(1,128)} %reshape.344), calls=%async_computation.19 | async-start | bytes 1572864 | tf_op jit(solution)/shard_map/all_to_all | solution.py:87
  1413.6 209.1 %all-reduce.25.cloned.1.call-start = ((), (), s32[]{:S(2)}) async-start(), calls=%async_computation.31 | async-start | bytes 3145728 | tf_op jit(solution)/shard_map/psum | solution.py:32
  1470.5 232.3 %all-gather.2.cloned.1.call-start = ((), (), s32[]{:S(2)}) async-start(), calls=%async_computation.32 | async-start | bytes 8912896 | tf_op jit(solution)/shard_map/all_gather | solution.py:148
  1492.6 16.6 all-to-all-start.23
  1501.1 335.0 %all-reduce.27.cloned.1.call-start = ((), (), s32[]{:S(2)}) async-start(), calls=%async_computation.33 | async-start | bytes 393216 | tf_op jit(solution)/shard_map/psum | solution.py:80
  1720.2 191.2 %all-to-all-start.21 = ((f32[16,2,3,8,128]{4,3,2,1,0:T(8,128)}), f32[16,2,3,8,128]{4,3,2,1,0:T(8,128)S(1)}, u32[]{:S(2)}, u32[]{:S(2)}) async-start(f32[16,2,3,8,128]{4,3,2,1,0:T(8,128)} %copy_bitcast_fusion.13), calls=%async_computation.21 | async-start | bytes 786432 | tf_op jit(solution)/shard_map/all_to_all | solution.py:43
  1723.8 185.9 %all-reduce.29.cloned.1.call-start = ((), (), s32[]{:S(2)}) async-start(), calls=%async_computation.34 | async-start | bytes 393216 | tf_op jit(solution)/shard_map/psum | solution.py:80
  (24 other events, 1113.3 us)
Sparse Core Ops, SparseCore 0:
  256.3 139.0 all-reduce.12
  397.9 72.4 all-reduce.14
  546.5 140.4 all-reduce.16
  692.2 145.6 all-reduce.10
  840.2 69.2 all-reduce.18
  952.8 152.4 all-reduce.20
  1192.0 146.2 all-reduce.22
  1470.6 151.9 all-reduce.24
  1624.9 77.8 all-gather.1
  1705.7 130.4 all-reduce.26
  1838.6 70.9 all-reduce.28
